TPU v7x, 128 devices: a whole 4x4x4 slice. The times are simulated.
128 devices in a mesh: pr: 16 (over z, x), pc: 8 (over y, core).
Axes of the slice: x: 4, y: 4, z: 4, core: 2. Of those that a mesh axis runs over, the one named last changes fastest.
Arguments:
- trailing: float32 [20480, 20480], P('pr', 'pc'), may hold values from -25 to 25, as said below
- v_panels: float32 [6, 32, 20480], P(None, None, ('pr', 'pc')), may hold values from -0.078125 to 0.078125
- t_panels: float32 [6, 32, 32], replicated, may hold values from -0.2 to 0.5, as said below
Outputs:
- updated: float32 [20480, 20480], P('pr', 'pc')
- w_panels: float32 [6, 32, 20480], P(None, None, ('pr', 'pc'))
Inputs may be any that keep to these rules, and one draw needn't show every extreme that they name: trailing is exactly symmetric. `t_panels`: each panel's factor is upper triangular with diagonal entries of 0.25 to 0.5.
All inputs are finite; a program needn't handle non-finite values.
Results may differ from a plain program's by a relative error of at most 0.00013.
Values sent between devices are 32-bit elements; how exact they have to be, the bound alone decides.
A program may use at most 128 MiB of HBM per device.

v0:
```python
import jax
import jax.numpy as jnp
from jax import lax
from jax.sharding import PartitionSpec as P

HIGHEST = lax.Precision.HIGHEST


def contract(left_side, right_side, left_dim, right_dim, precision=HIGHEST):
    return lax.dot_general(
        left_side,
        right_side,
        (((left_dim,), (right_dim,)), ((), ())),
        precision=precision,
        preferred_element_type=jnp.float32,
    )


def small_coefficients(gram_y, gram_v, t_panels):
    panels, width, _ = t_panels.shape
    size = panels * width
    eye = jnp.eye(size, dtype=jnp.float32)
    zero = jnp.zeros((size, size), jnp.float32)
    of_y = jnp.concatenate([gram_y, zero, eye], axis=1)
    of_v = jnp.concatenate([gram_v, eye, zero], axis=1)
    of_w = []
    for panel in range(panels):
        here = slice(panel * width, (panel + 1) * width)
        of_x = of_y[here]
        if panel:
            done = jnp.concatenate(of_w, axis=0)
            before = slice(0, panel * width)
            left = jnp.concatenate([done[:, here], gram_v[before, here]], axis=0)
            right = jnp.concatenate([of_v[before], done], axis=0)
            of_x = of_x - contract(left, right, 0, 0)
        factor = t_panels[panel]
        scaled = contract(factor, of_x, 0, 0)
        middle = contract(scaled[:, here], factor, 1, 0)
        of_w.append(scaled - 0.5 * contract(middle, of_v[here], 1, 0))
    return jnp.concatenate(of_w, axis=0)


def per_device(trailing, v_panels, t_panels):
    rows, cols = (lax.axis_size("pr"), lax.axis_size("pc"))
    ratio = rows // cols
    panels, width, share = v_panels.shape
    size = panels * width
    v_own = v_panels.reshape(size, share)
    moves = []
    for i in range(rows):
        for j in range(cols):
            moves.append((i * cols + j, (i % ratio * cols + j) * cols + i // ratio))

    def columns(own):
        return lax.all_gather(lax.ppermute(own, ("pr", "pc"), moves), "pr", axis=1, tiled=True)

    v_row = lax.all_gather(v_own, "pc", axis=1, tiled=True)
    v_col = columns(v_own)
    partial_y = contract(v_col, trailing, 1, 1, lax.Precision.HIGH)
    y_own = lax.psum_scatter(partial_y, "pc", scatter_dimension=1, tiled=True)
    y_row = lax.all_gather(y_own, "pc", axis=1, tiled=True)
    y_col = columns(y_own)
    grams = contract(v_own, jnp.concatenate([y_own, v_own], axis=0), 1, 1)
    grams = lax.psum(grams, ("pr", "pc"))
    coefs = small_coefficients(grams[:, :size], grams[:, size:], t_panels)
    of_v, of_y = (coefs[:, size : 2 * size], coefs[:, 2 * size :])
    w_own = contract(of_v, v_own, 1, 0) + contract(of_y, y_own, 1, 0)
    left_v = contract(of_v + of_v.T, v_row, 1, 0) + contract(of_y, y_row, 1, 0)
    left_y = contract(of_y, v_row, 0, 0)
    left = jnp.concatenate([left_v, left_y], axis=0)
    right = jnp.concatenate([v_col, y_col], axis=0)
    matrix = trailing - contract(left, right, 0, 0, lax.Precision.HIGH)
    return (matrix, w_own.reshape(panels, width, share))


def solution(mesh):
    return jax.shard_map(
        per_device,
        mesh=mesh,
        in_specs=(P("pr", "pc"), P(None, None, ("pr", "pc")), P()),
        out_specs=(P("pr", "pc"), P(None, None, ("pr", "pc"))),
        check_vma=False,
    )
```

profile of v0, /device:TPU:1, one launch (start us, length us, event | category | flops | bytes accessed | tf_op | source)
XLA Modules:
  0.0 353.8 jit_solution(15385846826090534265)
XLA Ops:
  7.2 1.0 copy.12
  8.2 4.5 %collective-permute-start = (f32[192,160]{0,1:T(8,128)S(1)}, f32[192,160]{0,1:T(8,128)S(1)}, u32[]{:S(2)}, u32[]{:S(2)}) collective-permute-start(f32[192,160]{0,1:T(8,128)S(1)} %copy.12), channel_id=1, source_target_pairs={{0,0},{1,8},{2,16},{3,24},{4,32},{5,40},{6,48},{7,56},{8,64},{9,72... | collective-permute-start | bytes 368648 | tf_op jit(solution)/shard_map/ppermute | solution.py:55
  12.8 4.5 %collective-permute-done = f32[192,160]{0,1:T(8,128)S(1)} collective-permute-done((f32[192,160]{0,1:T(8,128)S(1)}, f32[192,160]{0,1:T(8,128)S(1)}, u32[]{:S(2)}, u32[]{:S(2)}) %collective-permute-start) | collective-permute-done | bytes 122912 | tf_op jit(solution)/shard_map/ppermute | solution.py:55
  18.0 53.5 %all-gather.3.cloned.1.call-done = f32[192,2560]{0,1:T(8,128)} async-done(((f32[192,160]{0,1:T(8,128)}), f32[192,2560]{0,1:T(8,128)}) %all-gather.3.cloned.1.call-update) | async-done | bytes 1966096 | tf_op jit(solution)/shard_map/all_gather | solution.py:55
  71.5 9.9 %fusion.106 = f32[192,1280]{0,1:T(8,128)} fusion(f32[192,2560]{0,1:T(8,128)} %all-gather.3.cloned.1.call-done, f32[1280,2560]{1,0:T(8,128)} %param.3), kind=kOutput, calls=%fused_computation.158 | convolution fusion | flops 3774873600 | bytes 16056320 | tf_op jit(solution)/shard_map/dot_general | solution.py:10
  81.5 0.7 fusion.29
  82.2 15.8 %all_gather.13 = f32[192,1280]{0,1:T(8,128)S(1)} all-gather(f32[192,160]{0,1:T(8,128)S(1)} %copy.12), channel_id=1, replica_groups=mesh['pr'=16,'pc'=8] {'pc'}, dimensions={1}, use_global_device_ids=true | all-gather | bytes 1105920 | tf_op jit(solution)/shard_map/all_gather | solution.py:57
  98.0 13.6 %reduce-scatter.2.cloned.1.call-done = f32[192,160]{0,1:T(8,128)} async-done(((f32[192,1280]{0,1:T(8,128)}), f32[192,160]{0,1:T(8,128)}) %reduce-scatter.2.cloned.1.call-update) | async-done | bytes 122896 | tf_op jit(solution)/shard_map/reduce_scatter | solution.py:60
  111.6 2.2 convolution_bitcast_fusion
  113.9 6.3 %collective-permute-start.1 = (f32[192,160]{0,1:T(8,128)}, f32[192,160]{0,1:T(8,128)S(1)}, u32[]{:S(2)}, u32[]{:S(2)}) collective-permute-start(f32[192,160]{0,1:T(8,128)} %reduce-scatter.2.cloned.1.call-done), channel_id=1, source_target_pairs={{0,0},{1,8},{2,16},{3,24},{4,32},{5,40},{6,48},{7,56},{8,64},{9,72... | collective-permute-start | bytes 368648 | tf_op jit(solution)/shard_map/ppermute | solution.py:55
  120.2 20.7 %all_gather.14 = f32[192,1280]{0,1:T(8,128)S(1)} all-gather(f32[192,160]{0,1:T(8,128)} %reduce-scatter.2.cloned.1.call-done), channel_id=1, replica_groups=mesh['pr'=16,'pc'=8] {'pc'}, dimensions={1}, use_global_device_ids=true | all-gather | bytes 1105920 | tf_op jit(solution)/shard_map/all_gather | solution.py:61
  140.9 0.7 copy-done.4
  141.6 118.4 %all-reduce.2.cloned.1.call-done = f32[192,384]{1,0:T(8,128)} async-done(((f32[192,384]{1,0:T(8,128)}), f32[192,384]{1,0:T(8,128)}) %all-reduce.2.cloned.1.call-update) | async-done | bytes 294928 | tf_op jit(solution)/shard_map/psum | solution.py:64
  260.0 1.1 fusion.105
  261.2 2.0 pad_maximum_fusion.1
  263.2 0.7 slice.186
  263.9 0.7 slice.191
  264.6 0.8 slice_dynamic-update-slice_fusion.1
  265.4 0.8 slice_dynamic-update-slice_fusion
  266.1 0.8 slice.185
  267.6 0.9 slice.190
  268.5 0.7 copy.17
  269.1 1.2 convolution_bitcast_fusion.6
  270.3 0.9 fusion.66
  271.2 0.9 constant_dynamic-update-slice_fusion.8
  272.2 0.8 slice.181
  272.9 1.2 convolution_subtract_fusion.3
  274.1 1.0 convolution_bitcast_fusion.5
  275.1 0.9 fusion.64
  276.0 0.9 constant_dynamic-update-slice_fusion.7
  277.0 0.8 copy-done.6
  277.9 1.3 convolution_subtract_fusion.5
  279.2 1.0 convolution_bitcast_fusion.4
  280.2 0.9 fusion.62
  281.1 1.0 constant_dynamic-update-slice_fusion.6
  282.1 0.7 pad_maximum_fusion.5
  282.8 1.5 copy.16
  284.2 1.5 convolution_subtract_fusion.4
  285.8 1.0 convolution_bitcast_fusion.3
  287.4 1.5 fusion.60
  288.9 1.5 slice.195
  290.5 1.5 copy.19
  292.0 1.6 slice.201
  293.6 1.6 copy.21
  295.2 1.9 constant_dynamic-update-slice_fusion.5
  297.7 0.9 copy.18
  298.6 1.6 convolution_subtract_fusion.2
  300.2 1.0 convolution_bitcast_fusion.2
  301.2 0.9 fusion.58
  302.0 0.9 constant_dynamic-update-slice_fusion.4
  303.0 1.0 slice.200
  303.9 0.7 copy.20
  304.6 1.8 convolution_subtract_fusion.1
  306.4 1.0 convolution_bitcast_fusion.1
  307.4 0.9 fusion.56
  308.3 0.9 fusion.7
  309.2 1.1 slice.205
  310.3 1.3 fusion.30
  311.5 1.6 convolution_add_fusion.1
  313.1 0.8 copy.24
  314.0 3.9 %fusion.32 = f32[192,1280]{1,0:T(8,128)} fusion(f32[192,1280]{0,1:T(8,128)S(1)} %all_gather.13, f32[192,576]{1,0:T(8,128)} %fusion.7), kind=kOutput, calls=%fused_computation.59 | convolution fusion | flops 566231040 | bytes 2162688 | tf_op jit(solution)/shard_map/dot_general | solution.py:10
  317.9 2.4 fusion.28
  320.4 3.4 convolution_add_fusion
  323.8 23.5 %convolution_subtract_fusion = f32[1280,2560]{1,0:T(8,128)} fusion(f32[1280,2560]{1,0:T(8,128)} %param.3, f32[192,2560]{0,1:T(8,128)} %all-gather.5.cloned.1.call-done, f32[192,2560]{0,1:T(8,128)} %all-gather.3.cloned.1.call-done, f32[192,1280]{1,0:T(8,128)S(1)} %copy-done, f32[192,1280]{1,0:T(8,128)} %convolution_add_fusion), kind=kOutput, calls=%fused_computation | convolution fusion | flops 7554498560 | bytes 32112640 | tf_op jit(solution)/shard_map/dot_general | solution.py:10
  (30 shorter events, 3.2 us)
Async XLA Ops:
  7.2 64.3 %all-gather.3.cloned.1.call-start = ((), (), s32[]{:S(2)}) async-start(), calls=%async_computation.1 | async-start | bytes 2785280 | tf_op jit(solution)/shard_map/all_gather | solution.py:55
  8.2 9.0 %collective-permute-start = (f32[192,160]{0,1:T(8,128)S(1)}, f32[192,160]{0,1:T(8,128)S(1)}, u32[]{:S(2)}, u32[]{:S(2)}) collective-permute-start(f32[192,160]{0,1:T(8,128)S(1)} %copy.12), channel_id=1, source_target_pairs={{0,0},{1,8},{2,16},{3,24},{4,32},{5,40},{6,48},{7,56},{8,64},{9,72... | collective-permute-start | bytes 368648 | tf_op jit(solution)/shard_map/ppermute | solution.py:55
  17.3 0.7 copy-start.5
  18.0 93.6 %reduce-scatter.2.cloned.1.call-start = ((), (), s32[]{:S(2)}) async-start(), calls=%async_computation.2 | async-start | bytes 1474560 | tf_op jit(solution)/shard_map/reduce_scatter | solution.py:60
  81.4 30.2 %copy-start.1 = (f32[6,32,160]{2,1,0:T(8,128)S(1)}, f32[6,32,160]{2,1,0:T(8,128)}, u32[]{:S(2)}) copy-start(f32[6,32,160]{2,1,0:T(8,128)} %param.4) | copy-start | bytes 368644
  81.5 178.6 %all-reduce.2.cloned.1.call-start = ((), (), s32[]{:S(2)}) async-start(), calls=%async_computation.3 | async-start | bytes 589824 | tf_op jit(solution)/shard_map/psum | solution.py:64
  113.8 210.0 %all-gather.5.cloned.1.call-start = ((), (), s32[]{:S(2)}) async-start(), calls=%async_computation.4 | async-start | bytes 2785280 | tf_op jit(solution)/shard_map/all_gather | solution.py:55
  113.9 27.0 %collective-permute-start.1 = (f32[192,160]{0,1:T(8,128)}, f32[192,160]{0,1:T(8,128)S(1)}, u32[]{:S(2)}, u32[]{:S(2)}) collective-permute-start(f32[192,160]{0,1:T(8,128)} %reduce-scatter.2.cloned.1.call-done), channel_id=1, source_target_pairs={{0,0},{1,8},{2,16},{3,24},{4,32},{5,40},{6,48},{7,56},{8,64},{9,72... | collective-permute-start | bytes 368648 | tf_op jit(solution)/shard_map/ppermute | solution.py:55
  140.9 0.7 copy-start.4
  277.0 0.8 copy-start.6
  286.8 0.6 copy-start.3
  297.7 12.6 %copy-start.2 = (f32[192,160]{0,1:T(8,128)S(1)}, f32[192,160]{0,1:T(8,128)}, u32[]{:S(2)}) copy-start(f32[192,160]{0,1:T(8,128)} %reduce-scatter.2.cloned.1.call-done) | copy-start | bytes 368644
  320.3 3.4 copy-start
Sparse Core Ops, SparseCore 0:
  18.1 53.3 all-gather.2
  81.6 29.9 reduce-scatter.1
  116.9 143.0 all-reduce.1
  262.0 44.4 all-gather.4
where the time goes:
time: 355 us; the launch traced here: 354 us
  waiting for transfers between devices  190 us (54%)
  matrix products  74.1 us (21%)
  blocking collectives  36.6 us (10%)
  local copies, waits for them, and re-layouts  24.1 us (7%)
  between operations  14 us (4%)
  starting transfers between devices  11 us (3%)
  other arithmetic  4.12 us (1%)
    psum x1, waiting for transfers between devices, per_device(): grams = lax.psum(grams, ('pr', 'pc'))  118 us
    dot_general x31, matrix products, contract(): lax.dot_general(left_side, right_side, (((left_dim,), (right_dim,)), ((),...  74.1 us
    all_gather x2, waiting for transfers between devices, columns(): lax.all_gather(lax.ppermute(own, ('pr', 'pc'), moves), 'pr', axis=1, tile...  53.5 us
    all_gather x1, blocking collectives, per_device(): y_row = lax.all_gather(y_own, 'pc', axis=1, tiled=True)  20.7 us
    all_gather x1, blocking collectives, per_device(): v_row = lax.all_gather(v_own, 'pc', axis=1, tiled=True)  15.8 us
    slice x15, local copies, waits for them, and re-layouts, small_coefficients(): left = jnp.concatenate([done[:, here], gram_v[before, here]], axis=0)  14.3 us
    reduce_scatter x1, waiting for transfers between devices, per_device(): y_own = lax.psum_scatter(partial_y, 'pc', scatter_dimension=1, tiled=True)  13.6 us
    ppermute x2, starting transfers between devices, columns(): lax.ppermute(own, ('pr', 'pc'), moves)  10.8 us
  transfers between devices with their start and end apart: 6, of which 4 were waited for; matrix products, arithmetic and copies ran while one was open for 18% of the time, Pallas kernels for 0%

commit v1 on v0

--- a/solution.py
+++ b/solution.py
@@ -54,7 +54,12 @@
     def columns(own):
         return lax.all_gather(lax.ppermute(own, ("pr", "pc"), moves), "pr", axis=1, tiled=True)
 
-    v_row = lax.all_gather(v_own, "pc", axis=1, tiled=True)
+    ring = [v_own]
+    for hop in range(7):
+        ring.append(lax.ppermute(ring[-1], "pc", [(dev, (dev + 1) % 8) for dev in range(8)]))
+    v_row = jnp.roll(
+        jnp.concatenate(ring[::-1], axis=1), (lax.axis_index("pc") + 1) * ring[0].shape[1], axis=1
+    )
     v_col = columns(v_own)
     partial_y = contract(v_col, trailing, 1, 1, lax.Precision.HIGH)
     y_own = lax.psum_scatter(partial_y, "pc", scatter_dimension=1, tiled=True)

time: 355 us -> 351 us (0.989)
  blocking collectives: 36.6 us -> 20.2 us
  starting transfers between devices: 11 us -> 25.6 us
  waiting for transfers between devices: 190 us -> 202 us
  local copies, waits for them, and re-layouts: 24.1 us -> 16.1 us
  matrix products: 74.1 us -> 69 us
    ppermute x0 -> x7, waiting for transfers between devices: none -> 29.8 us  [per_device(): lax.ppermute(ring[-1], 'pc', [(dev, (dev + 1) % 8) for dev in range(8)])]
    all_gather x1 -> x0, blocking collectives: 15.8 us -> none  [per_device(): v_row = lax.all_gather(v_own, 'pc', axis=1, tiled=True)]
    reduce_scatter x1, waiting for transfers between devices: 13.6 us -> 0.02 us  [per_device(): y_own = lax.psum_scatter(partial_y, 'pc', scatter_dimension=1, tiled=True)]
    ppermute x0 -> x7, starting transfers between devices: none -> 13 us  [per_device(): lax.ppermute(ring[-1], 'pc', [(dev, (dev + 1) % 8) for dev in range(8)])]
    slice x15, local copies, waits for them, and re-layouts: 14.3 us -> 4.57 us  [small_coefficients(): left = jnp.concatenate([done[:, here], gram_v[before, here]], axis=0)]
    dot_general x31, matrix products: 74.1 us -> 69 us  [contract(): lax.dot_general(left_side, right_side, (((left_dim,), (right_dim,)), ((),...]
    psum x1, waiting for transfers between devices: 118 us -> 114 us  [per_device(): grams = lax.psum(grams, ('pr', 'pc'))]
  transfers between devices with their start and end apart: 6 -> 13, of which waited for: 4 -> 10; matrix products, arithmetic and copies ran while one was open for 18% -> 14% of each run, Pallas kernels for 0% -> 0%
where the time goes in v1:
time: 351 us; the launch traced here: 350 us
  waiting for transfers between devices  202 us (58%)
  matrix products  69 us (20%)
  starting transfers between devices  25.6 us (7%)
  blocking collectives  20.2 us (6%)
  local copies, waits for them, and re-layouts  16.1 us (5%)
  between operations  14 us (4%)
    psum x1, waiting for transfers between devices, per_device(): grams = lax.psum(grams, ('pr', 'pc'))  114 us
    dot_general x31, matrix products, contract(): lax.dot_general(left_side, right_side, (((left_dim,), (right_dim,)), ((),...  69 us
    all_gather x2, waiting for transfers between devices, columns(): lax.all_gather(lax.ppermute(own, ('pr', 'pc'), moves), 'pr', axis=1, tile...  53.5 us
    ppermute x7, waiting for transfers between devices, per_device(): lax.ppermute(ring[-1], 'pc', [(dev, (dev + 1) % 8) for dev in range(8)])  29.8 us
    all_gather x1, blocking collectives, per_device(): y_row = lax.all_gather(y_own, 'pc', axis=1, tiled=True)  20.2 us
    ppermute x7, starting transfers between devices, per_device(): lax.ppermute(ring[-1], 'pc', [(dev, (dev + 1) % 8) for dev in range(8)])  13 us
    ppermute x2, starting transfers between devices, columns(): lax.ppermute(own, ('pr', 'pc'), moves)  12.5 us
  transfers between devices with their start and end apart: 13, of which 10 were waited for; matrix products, arithmetic and copies ran while one was open for 14% of the time, Pallas kernels for 0%

profile of v1, /device:TPU:1, one launch (start us, length us, event | category | flops | bytes accessed | tf_op | source)
XLA Modules:
  0.0 349.7 jit_solution(13596898895503419526)
XLA Ops:
  7.2 1.0 copy.12
  8.3 4.5 %collective-permute-start = (f32[192,160]{0,1:T(8,128)S(1)}, f32[192,160]{0,1:T(8,128)S(1)}, u32[]{:S(2)}, u32[]{:S(2)}) collective-permute-start(f32[192,160]{0,1:T(8,128)S(1)} %copy.12), channel_id=1, source_target_pairs={{0,0},{1,8},{2,16},{3,24},{4,32},{5,40},{6,48},{7,56},{8,64},{9,72... | collective-permute-start | bytes 368648 | tf_op jit(solution)/shard_map/ppermute | solution.py:55
  12.8 4.5 %collective-permute-done = f32[192,160]{0,1:T(8,128)S(1)} collective-permute-done((f32[192,160]{0,1:T(8,128)S(1)}, f32[192,160]{0,1:T(8,128)S(1)}, u32[]{:S(2)}, u32[]{:S(2)}) %collective-permute-start) | collective-permute-done | bytes 122912 | tf_op jit(solution)/shard_map/ppermute | solution.py:55
  18.0 53.5 %all-gather.3.cloned.1.call-done = f32[192,2560]{0,1:T(8,128)} async-done(((f32[192,160]{0,1:T(8,128)}), f32[192,2560]{0,1:T(8,128)}) %all-gather.3.cloned.1.call-update) | async-done | bytes 1966096 | tf_op jit(solution)/shard_map/all_gather | solution.py:55
  71.5 9.9 %fusion.110 = f32[192,1280]{0,1:T(8,128)} fusion(f32[192,2560]{0,1:T(8,128)} %all-gather.3.cloned.1.call-done, f32[1280,2560]{1,0:T(8,128)} %param.3), kind=kOutput, calls=%fused_computation.162 | convolution fusion | flops 3774873600 | bytes 16056320 | tf_op jit(solution)/shard_map/dot_general | solution.py:10
  81.5 2.1 collective-permute-start.1
  83.6 2.6 collective-permute-done.1
  86.2 2.5 collective-permute-start.2
  88.7 3.5 collective-permute-done.2
  92.2 2.5 collective-permute-start.3
  94.7 3.5 collective-permute-done.3
  98.2 2.7 collective-permute-start.4
  100.9 4.2 %collective-permute-done.4 = f32[192,160]{1,0:T(8,128)S(1)} collective-permute-done((f32[192,160]{1,0:T(8,128)S(1)}, f32[192,160]{1,0:T(8,128)S(1)}, u32[]{:S(2)}, u32[]{:S(2)}) %collective-permute-start.4) | collective-permute-done | bytes 122912 | tf_op jit(solution)/shard_map/ppermute | solution.py:59
  105.1 2.3 collective-permute-start.5
  107.3 4.9 %collective-permute-done.5 = f32[192,160]{1,0:T(8,128)S(1)} collective-permute-done((f32[192,160]{1,0:T(8,128)S(1)}, f32[192,160]{1,0:T(8,128)S(1)}, u32[]{:S(2)}, u32[]{:S(2)}) %collective-permute-start.5) | collective-permute-done | bytes 122912 | tf_op jit(solution)/shard_map/ppermute | solution.py:59
  112.2 0.9 collective-permute-start.6
  113.2 5.4 %collective-permute-done.6 = f32[192,160]{1,0:T(8,128)S(1)} collective-permute-done((f32[192,160]{1,0:T(8,128)S(1)}, f32[192,160]{1,0:T(8,128)S(1)}, u32[]{:S(2)}, u32[]{:S(2)}) %collective-permute-start.6) | collective-permute-done | bytes 122912 | tf_op jit(solution)/shard_map/ppermute | solution.py:59
  118.6 0.7 fusion.31
  119.2 5.7 %collective-permute-done.7 = f32[192,160]{1,0:T(8,128)} collective-permute-done((f32[192,160]{1,0:T(8,128)S(1)}, f32[192,160]{1,0:T(8,128)}, u32[]{:S(2)}, u32[]{:S(2)}) %collective-permute-start.7) | collective-permute-done | bytes 122912 | tf_op jit(solution)/shard_map/ppermute | solution.py:59
  125.0 2.5 concatenate.88
  127.6 2.7 convolution_bitcast_fusion
  130.3 8.0 %collective-permute-start.8 = (f32[192,160]{0,1:T(8,128)}, f32[192,160]{0,1:T(8,128)S(1)}, u32[]{:S(2)}, u32[]{:S(2)}) collective-permute-start(f32[192,160]{0,1:T(8,128)} %reduce-scatter.2.cloned.1.call-done), channel_id=1, source_target_pairs={{0,0},{1,8},{2,16},{3,24},{4,32},{5,40},{6,48},{7,56},{8,64},{9,72... | collective-permute-start | bytes 368648 | tf_op jit(solution)/shard_map/ppermute | solution.py:55
  138.3 20.2 %all_gather.10 = f32[192,1280]{0,1:T(8,128)} all-gather(f32[192,160]{0,1:T(8,128)} %reduce-scatter.2.cloned.1.call-done), channel_id=1, replica_groups=mesh['pr'=16,'pc'=8] {'pc'}, dimensions={1}, use_global_device_ids=true | all-gather | bytes 1105920 | tf_op jit(solution)/shard_map/all_gather | solution.py:66
  159.2 114.1 %all-reduce.2.cloned.1.call-done = f32[192,384]{1,0:T(8,128)} async-done(((f32[192,384]{1,0:T(8,128)}), f32[192,384]{1,0:T(8,128)}) %all-reduce.2.cloned.1.call-update) | async-done | bytes 294928 | tf_op jit(solution)/shard_map/psum | solution.py:69
  273.3 1.2 fusion.109
  274.6 1.2 pad_maximum_fusion.1
  275.8 0.7 slice.178
  276.5 0.7 slice.186
  277.2 0.7 slice.191
  277.9 0.7 slice_dynamic-update-slice_fusion.1
  278.6 0.8 slice_dynamic-update-slice_fusion
  279.6 0.7 copy.17
  280.3 0.7 copy.19
  281.1 0.7 copy.21
  281.8 1.0 convolution_bitcast_fusion.6
  282.8 0.9 fusion.68
  283.6 0.9 constant_dynamic-update-slice_fusion.8
  284.7 1.2 convolution_subtract_fusion.3
  285.9 1.0 convolution_bitcast_fusion.5
  286.9 0.9 fusion.66
  287.8 0.9 constant_dynamic-update-slice_fusion.7
  288.8 0.8 copy-done.9
  289.7 1.3 convolution_subtract_fusion.5
  291.0 1.0 convolution_bitcast_fusion.4
  292.0 0.9 fusion.64
  292.9 0.9 constant_dynamic-update-slice_fusion.6
  294.1 1.5 convolution_subtract_fusion.4
  295.6 1.0 convolution_bitcast_fusion.3
  296.6 0.9 fusion.62
  297.5 1.0 constant_dynamic-update-slice_fusion.5
  299.1 0.9 copy.18
  300.0 1.6 convolution_subtract_fusion.2
  301.6 1.0 convolution_bitcast_fusion.2
  302.6 0.9 fusion.60
  303.4 0.9 constant_dynamic-update-slice_fusion.4
  304.3 1.0 slice.200
  305.3 1.7 convolution_subtract_fusion.1
  307.1 1.0 convolution_bitcast_fusion.1
  308.1 0.9 fusion.58
  310.3 0.8 copy.23
  311.2 2.2 fusion.13
  313.5 2.9 fusion.35
  316.4 3.4 convolution_add_fusion
  319.8 23.4 %convolution_subtract_fusion = f32[1280,2560]{1,0:T(8,128)} fusion(f32[1280,2560]{1,0:T(8,128)} %param.3, f32[192,2560]{0,1:T(8,128)} %all-gather.5.cloned.1.call-done, f32[192,2560]{0,1:T(8,128)S(1)} %copy-done, f32[192,1280]{1,0:T(8,128)} %fusion.13, f32[192,1280]{1,0:T(8,128)} %convolution_add_fusion), kind=kOutput, calls=%fused_computation | convolution fusion | flops 7554498560 | bytes 32112640 | tf_op jit(solution)/shard_map/dot_general | solution.py:10
  (52 shorter events, 4.5 us)
Async XLA Ops:
  7.2 64.3 %all-gather.3.cloned.1.call-start = ((), (), s32[]{:S(2)}) async-start(), calls=%async_computation.1 | async-start | bytes 2785280 | tf_op jit(solution)/shard_map/all_gather | solution.py:55
  8.2 73.2 %copy-start.6 = (f32[192,160]{0,1:T(8,128)}, f32[192,160]{0,1:T(8,128)S(1)}, u32[]{:S(2)}) copy-start(f32[192,160]{0,1:T(8,128)S(1)} %copy.12) | copy-start | bytes 368644
  8.3 9.0 %collective-permute-start = (f32[192,160]{0,1:T(8,128)S(1)}, f32[192,160]{0,1:T(8,128)S(1)}, u32[]{:S(2)}, u32[]{:S(2)}) collective-permute-start(f32[192,160]{0,1:T(8,128)S(1)} %copy.12), channel_id=1, source_target_pairs={{0,0},{1,8},{2,16},{3,24},{4,32},{5,40},{6,48},{7,56},{8,64},{9,72... | collective-permute-start | bytes 368648 | tf_op jit(solution)/shard_map/ppermute | solution.py:55
  17.3 0.7 copy-start.8
  18.0 63.5 %copy-start.2 = (f32[6,32,160]{2,1,0:T(8,128)S(1)}, f32[6,32,160]{2,1,0:T(8,128)}, u32[]{:S(2)}) copy-start(f32[6,32,160]{2,1,0:T(8,128)} %param.4) | copy-start | bytes 368644
  18.0 109.6 %reduce-scatter.2.cloned.1.call-start = ((), (), s32[]{:S(2)}) async-start(), calls=%async_computation.2 | async-start | bytes 1474560 | tf_op jit(solution)/shard_map/reduce_scatter | solution.py:65
  81.5 191.9 %all-reduce.2.cloned.1.call-start = ((), (), s32[]{:S(2)}) async-start(), calls=%async_computation.3 | async-start | bytes 589824 | tf_op jit(solution)/shard_map/psum | solution.py:69
  81.5 4.7 %collective-permute-start.1 = (f32[192,160]{1,0:T(8,128)S(1)}, f32[192,160]{1,0:T(8,128)S(1)}, u32[]{:S(2)}, u32[]{:S(2)}) collective-permute-start(f32[192,160]{1,0:T(8,128)S(1)} %bitcast.69), channel_id=1, source_target_pairs={{0,1},{1,2},{2,3},{3,4},{4,5},{5,6},{6,7},{7,0},{8,9},{9,10},{10,1... | collective-permute-start | bytes 368648 | tf_op jit(solution)/shard_map/ppermute | solution.py:59
  86.2 6.0 %collective-permute-start.2 = (f32[192,160]{1,0:T(8,128)S(1)}, f32[192,160]{1,0:T(8,128)S(1)}, u32[]{:S(2)}, u32[]{:S(2)}) collective-permute-start(f32[192,160]{1,0:T(8,128)S(1)} %collective-permute-done.1), channel_id=1, source_target_pairs={{0,1},{1,2},{2,3},{3,4},{4,5},{5,6},{6,7},{7,0},{8,9},{9,10},{10,1... | collective-permute-start | bytes 368648 | tf_op jit(solution)/shard_map/ppermute | solution.py:59
  92.2 6.0 %collective-permute-start.3 = (f32[192,160]{1,0:T(8,128)S(1)}, f32[192,160]{1,0:T(8,128)S(1)}, u32[]{:S(2)}, u32[]{:S(2)}) collective-permute-start(f32[192,160]{1,0:T(8,128)S(1)} %collective-permute-done.2), channel_id=1, source_target_pairs={{0,1},{1,2},{2,3},{3,4},{4,5},{5,6},{6,7},{7,0},{8,9},{9,10},{10,1... | collective-permute-start | bytes 368648 | tf_op jit(solution)/shard_map/ppermute | solution.py:59
  98.2 6.9 %collective-permute-start.4 = (f32[192,160]{1,0:T(8,128)S(1)}, f32[192,160]{1,0:T(8,128)S(1)}, u32[]{:S(2)}, u32[]{:S(2)}) collective-permute-start(f32[192,160]{1,0:T(8,128)S(1)} %collective-permute-done.3), channel_id=1, source_target_pairs={{0,1},{1,2},{2,3},{3,4},{4,5},{5,6},{6,7},{7,0},{8,9},{9,10},{10,1... | collective-permute-start | bytes 368648 | tf_op jit(solution)/shard_map/ppermute | solution.py:59
  105.1 7.2 %collective-permute-start.5 = (f32[192,160]{1,0:T(8,128)S(1)}, f32[192,160]{1,0:T(8,128)S(1)}, u32[]{:S(2)}, u32[]{:S(2)}) collective-permute-start(f32[192,160]{1,0:T(8,128)S(1)} %collective-permute-done.4), channel_id=1, source_target_pairs={{0,1},{1,2},{2,3},{3,4},{4,5},{5,6},{6,7},{7,0},{8,9},{9,10},{10,1... | collective-permute-start | bytes 368648 | tf_op jit(solution)/shard_map/ppermute | solution.py:59
  112.2 6.3 %collective-permute-start.6 = (f32[192,160]{1,0:T(8,128)S(1)}, f32[192,160]{1,0:T(8,128)S(1)}, u32[]{:S(2)}, u32[]{:S(2)}) collective-permute-start(f32[192,160]{1,0:T(8,128)S(1)} %collective-permute-done.5), channel_id=1, source_target_pairs={{0,1},{1,2},{2,3},{3,4},{4,5},{5,6},{6,7},{7,0},{8,9},{9,10},{10,1... | collective-permute-start | bytes 368648 | tf_op jit(solution)/shard_map/ppermute | solution.py:59
  118.6 6.4 %collective-permute-start.7 = (f32[192,160]{1,0:T(8,128)S(1)}, f32[192,160]{1,0:T(8,128)}, u32[]{:S(2)}, u32[]{:S(2)}) collective-permute-start(f32[192,160]{1,0:T(8,128)S(1)} %collective-permute-done.6), channel_id=1, source_target_pairs={{0,1},{1,2},{2,3},{3,4},{4,5},{5,6},{6,7},{7,0},{8,9},{9,10},{10,1... | collective-permute-start | bytes 368648 | tf_op jit(solution)/shard_map/ppermute | solution.py:59
  127.5 183.7 %copy-start.1 = (f32[192,2560]{1,0:T(8,128)}, f32[192,2560]{1,0:T(8,128)S(1)}, u32[]{:S(2)}) copy-start(f32[192,2560]{1,0:T(8,128)S(1)} %concatenate.88) | copy-start | bytes 5898244
  130.3 189.5 %all-gather.5.cloned.1.call-start = ((), (), s32[]{:S(2)}) async-start(), calls=%async_computation.4 | async-start | bytes 2785280 | tf_op jit(solution)/shard_map/all_gather | solution.py:55
  130.3 28.2 %collective-permute-start.8 = (f32[192,160]{0,1:T(8,128)}, f32[192,160]{0,1:T(8,128)S(1)}, u32[]{:S(2)}, u32[]{:S(2)}) collective-permute-start(f32[192,160]{0,1:T(8,128)} %reduce-scatter.2.cloned.1.call-done), channel_id=1, source_target_pairs={{0,0},{1,8},{2,16},{3,24},{4,32},{5,40},{6,48},{7,56},{8,64},{9,72... | collective-permute-start | bytes 368648 | tf_op jit(solution)/shard_map/ppermute | solution.py:55
  158.5 0.7 copy-start.7
  273.3 6.1 %copy-start.5 = (f32[192,384]{1,0:T(8,128)S(1)}, f32[192,384]{1,0:T(8,128)}, u32[]{:S(2)}) copy-start(f32[192,384]{1,0:T(8,128)} %all-reduce.2.cloned.1.call-done) | copy-start | bytes 884740
  275.8 7.0 %copy-start.3 = (f32[192,576]{1,0:T(8,128)}, f32[192,576]{1,0:T(8,128)S(1)}, u32[]{:S(2)}) copy-start(f32[192,576]{1,0:T(8,128)S(1)} %get-tuple-element.5) | copy-start | bytes 1327108
  284.7 9.4 %copy-start.10 = (f32[96,32]{0,1:T(8,128)S(1)}, f32[96,32]{0,1:T(8,128)}, u32[]{:S(2)}) copy-start(f32[96,32]{0,1:T(8,128)} %copy.17) | copy-start | bytes 36868
  288.8 0.8 copy-start.9
  295.5 13.8 %copy-start.4 = (f32[192,160]{0,1:T(8,128)S(1)}, f32[192,160]{0,1:T(8,128)}, u32[]{:S(2)}) copy-start(f32[192,160]{0,1:T(8,128)} %reduce-scatter.2.cloned.1.call-done) | copy-start | bytes 368644
  313.5 6.3 %copy-start = (f32[192,2560]{0,1:T(8,128)S(1)}, f32[192,2560]{0,1:T(8,128)}, u32[]{:S(2)}) copy-start(f32[192,2560]{0,1:T(8,128)} %all-gather.3.cloned.1.call-done) | copy-start | bytes 5898244
Sparse Core Ops, SparseCore 0:
  18.1 53.3 all-gather.2
  81.6 30.1 reduce-scatter.1
  130.4 142.8 all-reduce.1
  275.3 44.3 all-gather.4
